TPU v7x, 32 devices: a whole 2x2x4 slice. The times are simulated.
32 devices in a mesh: section: 4 (over x, core), ep: 8 (over z, y).
Axes of the slice: x: 2, y: 2, z: 4, core: 2. Of those that a mesh axis runs over, the one named last changes fastest.
Arguments:
- hidden: bfloat16 [1024, 4096], P(('section', 'ep')), may hold values from -6 to 6
- route_ids: int32 [4, 1024, 8], P(None, ('section', 'ep')), may hold values from 0 to 127, all different within a row; in each aligned block of 32 rows (0 to 31, 32 to 63, ..., all dimensions but the last counted through in order) at most 4 rows name the same one
- route_logits: float32 [4, 1024, 8], P(None, ('section', 'ep')), may hold values from -4 to 4
- norm_gain: bfloat16 [4, 4096], P('section'), may hold values from 0.099609375 to 1.8984375
- w_gate: bfloat16 [4, 3072, 4096], P('section', 'ep'), may hold values from -0.09375 to 0.09375
- w_up: bfloat16 [4, 3072, 4096], P('section', 'ep'), may hold values from -0.09375 to 0.09375
- w_down: bfloat16 [4, 3072, 4096], P('section', 'ep'), may hold values from -0.625 to 0.625
Outputs:
- final_hidden: bfloat16 [1024, 4096], P(('section', 'ep'))
Inputs may be any that keep to these rules, and one draw needn't show every extreme that they name: `route_ids`: in each tick, at most 4 of the 32 rows of one device name any one expert; each row names 8 different experts.
All inputs are finite; a program needn't handle non-finite values.
Results may differ from a plain program's by a relative error of at most 0.0043.
Values may be sent and summed in bfloat16 or wider, within the bound.
A program may use at most 64 MiB of HBM per device.

v0:
```python
import jax
import jax.numpy as jnp
from jax import lax
from jax.sharding import PartitionSpec as P

FE = 1536
MOST = 4


def shifted(x, axis, by):
    peers = lax.axis_size(axis)
    return lax.ppermute(x, axis, [(i, (i + by) % peers) for i in range(peers)])


def project_rows(rows, weight_t):
    return lax.dot_general(
        rows, weight_t, (((1,), (1,)), ((), ())), preferred_element_type=jnp.float32
    )


def expert_part(rows, wg, wu, wd):
    gate = project_rows(rows, wg)
    upper = project_rows(rows, wu)
    act = (jax.nn.silu(gate) * upper).astype(jnp.bfloat16)
    return jnp.dot(act, wd, preferred_element_type=jnp.float32)


def shards(hidden, route_ids, route_logits, norm_gain, w_gate, w_up, w_down):
    wg_mine = w_gate[0]
    wu_mine = w_up[0]
    wd_mine = w_down[0]
    gain = norm_gain[0].astype(jnp.float32)
    rows_dev = hidden.shape[0]
    width = hidden.shape[1]
    units = wg_mine.shape[0]
    sharers = FE // units
    ep_count = lax.axis_size("ep")
    held = ep_count // sharers
    state = hidden
    for tick in range(route_ids.shape[0]):
        ids = route_ids[tick]
        logits = route_logits[tick]
        hf = state.astype(jnp.float32)
        msq = jnp.mean(hf * hf, axis=-1, keepdims=True) + 1e-06
        normed = (hf * lax.rsqrt(msq) * gain).astype(jnp.bfloat16)
        expo = jnp.exp(logits)
        probs = expo / jnp.sum(expo, axis=-1, keepdims=True)
        matches = [ids == j for j in range(held)]
        weight_cols = jnp.stack(
            [jnp.sum(jnp.where(m, probs, 0.0), axis=-1) for m in matches], axis=1
        ).astype(jnp.bfloat16)
        orders = []
        picked = []
        slot_cols = []
        for j in range(held):
            hits = jnp.any(matches[j], axis=-1).astype(jnp.int32)
            order = jnp.argsort(1 - hits, stable=True)[:MOST]
            valid = jnp.arange(MOST, dtype=jnp.int32) < jnp.sum(hits)
            orders.append(order)
            picked.append(normed[order])
            slot_cols.append(jnp.where(valid, weight_cols[order, j], jnp.zeros((), jnp.bfloat16)))
        slot_rows = jnp.stack(picked, axis=0)
        outgoing = jnp.repeat(slot_rows, sharers, axis=0)
        block = lax.all_to_all(outgoing, "ep", split_axis=0, concat_axis=0, tiled=True)
        senders = block.shape[0]
        slots = block.shape[1]
        flat = block.reshape(senders * slots, width)
        partial_sums = expert_part(flat, wg_mine, wu_mine, wd_mine).reshape(senders, slots, width)
        returned = lax.all_to_all(partial_sums, "ep", split_axis=0, concat_axis=0, tiled=True)
        expert_sums = jnp.sum(returned.reshape(held, sharers, MOST, width), axis=1)
        slot_weights = jnp.stack(slot_cols, axis=0).astype(jnp.float32)
        weighted = slot_weights[:, :, None] * expert_sums
        order_all = jnp.stack(orders, axis=0)
        placing = (
            order_all[:, :, None] == jnp.arange(rows_dev, dtype=jnp.int32)[None, None, :]
        ).astype(jnp.float32)
        summed = jnp.einsum("jmr,jmd->rd", placing, weighted, precision=lax.Precision.HIGHEST)
        out = (hf + summed).astype(jnp.bfloat16)
        state = shifted(out, "section", 1)
    return state


def solution(mesh):
    placed = (
        P(("section", "ep"), None),
        P(None, ("section", "ep"), None),
        P(None, ("section", "ep"), None),
        P("section", None),
        P("section", "ep", None),
        P("section", "ep", None),
        P("section", "ep", None),
    )
    return jax.shard_map(
        shards, mesh=mesh, in_specs=placed, out_specs=P(("section", "ep"), None), check_vma=False
    )
```

profile of v0, /device:TPU:0, one launch (start us, length us, event | category | flops | bytes accessed | tf_op | source)
XLA Modules:
  0.0 209.3 jit_solution(5921479602172409629)
XLA Ops:
  3.9 1.7 sort.115
  6.2 1.7 sort.116
  12.1 16.1 %all_to_all.40 = bf16[8,4,4096]{2,1,0:T(4,128)(2,1)} all-to-all(bf16[8,4,4096]{2,1,0:T(4,128)(2,1)S(1)} %bitcast.198), channel_id=1, replica_groups=mesh['section'=4,'ep'=8] {'ep'}, dimensions={0} | all-to-all | bytes 524288 | tf_op jit(solution)/shard_map/all_to_all | solution.py:64
  29.3 3.1 %fusion.30 = f32[32,384]{1,0:T(8,128)S(1)} fusion(bf16[32,4096]{1,0:T(8,128)(2,1)S(1)} %reshape.285, bf16[1,384,4096]{2,1,0:T(8,128)(2,1)} %param.11), kind=kOutput, calls=%fused_computation.50 | convolution fusion | flops 100663296 | bytes 3457024 | tf_op jit(solution)/shard_map/dot_general | solution.py:16
  34.9 4.1 %all-to-all-start.1 = ((f32[8,4,4096]{2,1,0:T(4,128)}), f32[8,4,4096]{2,1,0:T(4,128)}, u32[]{:S(2)}, u32[]{:S(2)}) async-start(f32[8,4,4096]{2,1,0:T(4,128)} %fusion.14), calls=%async_computation.1 | async-start | bytes 1048576 | tf_op jit(solution)/shard_map/all_to_all | solution.py:69
  42.4 1.6 sort.117
  44.0 1.6 sort.118
  45.6 7.1 %all-to-all-done.1 = f32[8,4,4096]{2,1,0:T(4,128)} async-done(((f32[8,4,4096]{2,1,0:T(4,128)}), f32[8,4,4096]{2,1,0:T(4,128)}, u32[]{:S(2)}, u32[]{:S(2)}) %all-to-all-start.1) | async-done | bytes 524320 | tf_op jit(solution)/shard_map/all_to_all | solution.py:69
  54.7 5.7 %collective-permute-done = bf16[32,4096]{1,0:T(8,128)(2,1)S(1)} collective-permute-done((bf16[32,4096]{1,0:T(8,128)(2,1)S(1)}, bf16[32,4096]{1,0:T(8,128)(2,1)S(1)}, u32[]{:S(2)}, u32[]{:S(2)}) %collective-permute-start) | collective-permute-done | bytes 262176 | tf_op jit(solution)/shard_map/ppermute | solution.py:12
  65.5 4.0 %all-to-all-start.2 = ((bf16[8,4,4096]{2,1,0:T(4,128)(2,1)}), bf16[8,4,4096]{2,1,0:T(4,128)(2,1)}, u32[]{:S(2)}, u32[]{:S(2)}) async-start(bf16[8,4,4096]{2,1,0:T(4,128)(2,1)} %bitcast.197), calls=%async_computation.2 | async-start | bytes 524288 | tf_op jit(solution)/shard_map/all_to_all | solution.py:64
  72.2 5.9 %all-to-all-done.2 = bf16[8,4,4096]{2,1,0:T(4,128)(2,1)} async-done(((bf16[8,4,4096]{2,1,0:T(4,128)(2,1)}), bf16[8,4,4096]{2,1,0:T(4,128)(2,1)}, u32[]{:S(2)}, u32[]{:S(2)}) %all-to-all-start.2) | async-done | bytes 262176 | tf_op jit(solution)/shard_map/all_to_all | solution.py:64
  78.1 1.7 reshape.288
  79.8 3.2 %fusion.28 = f32[32,384]{1,0:T(8,128)S(1)} fusion(bf16[32,4096]{1,0:T(8,128)(2,1)} %reshape.288, bf16[1,384,4096]{2,1,0:T(8,128)(2,1)} %param.11), kind=kOutput, calls=%fused_computation.48 | convolution fusion | flops 100663296 | bytes 3457024 | tf_op jit(solution)/shard_map/dot_general | solution.py:16
  85.5 4.1 %all-to-all-start.3 = ((f32[8,4,4096]{2,1,0:T(4,128)}), f32[8,4,4096]{2,1,0:T(4,128)}, u32[]{:S(2)}, u32[]{:S(2)}) async-start(f32[8,4,4096]{2,1,0:T(4,128)} %fusion.12), calls=%async_computation.3 | async-start | bytes 1048576 | tf_op jit(solution)/shard_map/all_to_all | solution.py:69
  91.1 1.6 sort.119
  93.4 1.6 sort.120
  95.0 8.2 %all-to-all-done.3 = f32[8,4,4096]{2,1,0:T(4,128)} async-done(((f32[8,4,4096]{2,1,0:T(4,128)}), f32[8,4,4096]{2,1,0:T(4,128)}, u32[]{:S(2)}, u32[]{:S(2)}) %all-to-all-start.3) | async-done | bytes 524320 | tf_op jit(solution)/shard_map/all_to_all | solution.py:69
  105.1 5.7 %collective-permute-done.1 = bf16[32,4096]{1,0:T(8,128)(2,1)S(1)} collective-permute-done((bf16[32,4096]{1,0:T(8,128)(2,1)S(1)}, bf16[32,4096]{1,0:T(8,128)(2,1)S(1)}, u32[]{:S(2)}, u32[]{:S(2)}) %collective-permute-start.1) | collective-permute-done | bytes 262176 | tf_op jit(solution)/shard_map/ppermute | solution.py:12
  115.2 11.8 %all_to_all.41 = bf16[8,4,4096]{2,1,0:T(4,128)(2,1)} all-to-all(bf16[8,4,4096]{2,1,0:T(4,128)(2,1)S(1)} %bitcast.199), channel_id=1, replica_groups=mesh['section'=4,'ep'=8] {'ep'}, dimensions={0} | all-to-all | bytes 524288 | tf_op jit(solution)/shard_map/all_to_all | solution.py:64
  127.0 1.7 reshape.291
  128.8 3.2 %fusion.26 = f32[32,384]{1,0:T(8,128)S(1)} fusion(bf16[32,4096]{1,0:T(8,128)(2,1)} %reshape.291, bf16[1,384,4096]{2,1,0:T(8,128)(2,1)} %param.11), kind=kOutput, calls=%fused_computation.46 | convolution fusion | flops 100663296 | bytes 3457024 | tf_op jit(solution)/shard_map/dot_general | solution.py:16
  134.4 4.3 %all-to-all-start.5 = ((f32[8,4,4096]{2,1,0:T(4,128)}), f32[8,4,4096]{2,1,0:T(4,128)}, u32[]{:S(2)}, u32[]{:S(2)}) async-start(f32[8,4,4096]{2,1,0:T(4,128)} %fusion.10), calls=%async_computation.5 | async-start | bytes 1048576 | tf_op jit(solution)/shard_map/all_to_all | solution.py:69
  142.1 1.6 sort.121
  143.7 1.6 sort.122
  145.4 4.0 %all-to-all-done.5 = f32[8,4,4096]{2,1,0:T(4,128)} async-done(((f32[8,4,4096]{2,1,0:T(4,128)}), f32[8,4,4096]{2,1,0:T(4,128)}, u32[]{:S(2)}, u32[]{:S(2)}) %all-to-all-start.5) | async-done | bytes 524320 | tf_op jit(solution)/shard_map/all_to_all | solution.py:69
  151.3 5.7 %collective-permute-done.2 = bf16[32,4096]{1,0:T(8,128)(2,1)S(1)} collective-permute-done((bf16[32,4096]{1,0:T(8,128)(2,1)S(1)}, bf16[32,4096]{1,0:T(8,128)(2,1)S(1)}, u32[]{:S(2)}, u32[]{:S(2)}) %collective-permute-start.2) | collective-permute-done | bytes 262176 | tf_op jit(solution)/shard_map/ppermute | solution.py:12
  161.4 13.7 %all_to_all.42 = bf16[8,4,4096]{2,1,0:T(4,128)(2,1)} all-to-all(bf16[8,4,4096]{2,1,0:T(4,128)(2,1)S(1)} %bitcast.200), channel_id=1, replica_groups=mesh['section'=4,'ep'=8] {'ep'}, dimensions={0} | all-to-all | bytes 524288 | tf_op jit(solution)/shard_map/all_to_all | solution.py:64
  175.1 1.7 reshape.294
  176.8 3.2 %fusion.24 = f32[32,384]{1,0:T(8,128)S(1)} fusion(bf16[32,4096]{1,0:T(8,128)(2,1)} %reshape.294, bf16[1,384,4096]{2,1,0:T(8,128)(2,1)} %param.11), kind=kOutput, calls=%fused_computation.44 | convolution fusion | flops 100663296 | bytes 3457024 | tf_op jit(solution)/shard_map/dot_general | solution.py:16
  182.5 4.1 %all-to-all-start.7 = ((f32[8,4,4096]{2,1,0:T(4,128)}), f32[8,4,4096]{2,1,0:T(4,128)}, u32[]{:S(2)}, u32[]{:S(2)}) async-start(f32[8,4,4096]{2,1,0:T(4,128)} %fusion.8), calls=%async_computation.7 | async-start | bytes 1048576 | tf_op jit(solution)/shard_map/all_to_all | solution.py:69
  189.3 11.6 %all-to-all-done.7 = f32[8,4,4096]{2,1,0:T(4,128)} async-done(((f32[8,4,4096]{2,1,0:T(4,128)}), f32[8,4,4096]{2,1,0:T(4,128)}, u32[]{:S(2)}, u32[]{:S(2)}) %all-to-all-start.7) | async-done | bytes 524320 | tf_op jit(solution)/shard_map/all_to_all | solution.py:69
  202.8 5.8 %collective-permute-done.3 = bf16[32,4096]{1,0:T(8,128)(2,1)S(1)} collective-permute-done((bf16[32,4096]{1,0:T(8,128)(2,1)S(1)}, bf16[32,4096]{1,0:T(8,128)(2,1)S(1)}, u32[]{:S(2)}, u32[]{:S(2)}) %collective-permute-start.3) | collective-permute-done | bytes 262176 | tf_op jit(solution)/shard_map/ppermute | solution.py:12
  (148 shorter events, 55.8 us)
Async XLA Ops:
  0.0 33.5 %copy-start = (bf16[1,384,4096]{2,1,0:T(8,128)(2,1)S(1)}, bf16[1,384,4096]{2,1,0:T(8,128)(2,1)}, u32[]{:S(2)}) copy-start(bf16[1,384,4096]{2,1,0:T(8,128)(2,1)} %param.13) | copy-start | bytes 9437188
  29.3 3.1 %copy-start.1 = (bf16[1,384,4096]{2,1,0:T(8,128)(2,1)S(1)}, bf16[1,384,4096]{2,1,0:T(8,128)(2,1)}, u32[]{:S(2)}) copy-start(bf16[1,384,4096]{2,1,0:T(8,128)(2,1)} %param.12) | copy-start | bytes 9437188
  33.4 5.6 %copy-start.9 = (bf16[32]{0:T(256)(128)(2,1)S(1)}, bf16[32]{0:T(256)(128)(2,1)}, u32[]{:S(2)}) copy-start(bf16[32]{0:T(256)(128)(2,1)} %get-tuple-element.65) | copy-start | bytes 196
  33.5 5.6 %copy-start.10 = (bf16[32]{0:T(256)(128)(2,1)S(1)}, bf16[32]{0:T(256)(128)(2,1)}, u32[]{:S(2)}) copy-start(bf16[32]{0:T(256)(128)(2,1)} %get-tuple-element.67) | copy-start | bytes 196
  33.5 20.6 %copy-start.5 = (bf16[32,4096]{1,0:T(8,128)(2,1)S(1)}, bf16[32,4096]{1,0:T(8,128)(2,1)}, u32[]{:S(2)}) copy-start(bf16[32,4096]{1,0:T(8,128)(2,1)} %param.7) | copy-start | bytes 786436
  34.9 17.9 %all-to-all-start.1 = ((f32[8,4,4096]{2,1,0:T(4,128)}), f32[8,4,4096]{2,1,0:T(4,128)}, u32[]{:S(2)}, u32[]{:S(2)}) async-start(f32[8,4,4096]{2,1,0:T(4,128)} %fusion.14), calls=%async_computation.1 | async-start | bytes 1048576 | tf_op jit(solution)/shard_map/all_to_all | solution.py:69
  54.6 5.8 %collective-permute-start = (bf16[32,4096]{1,0:T(8,128)(2,1)S(1)}, bf16[32,4096]{1,0:T(8,128)(2,1)S(1)}, u32[]{:S(2)}, u32[]{:S(2)}) collective-permute-start(bf16[32,4096]{1,0:T(8,128)(2,1)S(1)} %fusion.7), channel_id=1, source_target_pairs={{0,8},{8,16},{16,24},{24,0},{1,9},{9,17},{17,25},{25,1},{2,10},{10... | collective-permute-start | bytes 786440 | tf_op jit(solution)/shard_map/ppermute | solution.py:12
  65.5 12.6 %all-to-all-start.2 = ((bf16[8,4,4096]{2,1,0:T(4,128)(2,1)}), bf16[8,4,4096]{2,1,0:T(4,128)(2,1)}, u32[]{:S(2)}, u32[]{:S(2)}) async-start(bf16[8,4,4096]{2,1,0:T(4,128)(2,1)} %bitcast.197), calls=%async_computation.2 | async-start | bytes 524288 | tf_op jit(solution)/shard_map/all_to_all | solution.py:64
  79.8 3.2 %copy-start.2 = (bf16[1,384,4096]{2,1,0:T(8,128)(2,1)S(1)}, bf16[1,384,4096]{2,1,0:T(8,128)(2,1)}, u32[]{:S(2)}) copy-start(bf16[1,384,4096]{2,1,0:T(8,128)(2,1)} %param.12) | copy-start | bytes 9437188
  79.8 3.2 %copy-start.6 = (bf16[32,4096]{1,0:T(8,128)(2,1)S(1)}, bf16[32,4096]{1,0:T(8,128)(2,1)}, u32[]{:S(2)}) copy-start(bf16[32,4096]{1,0:T(8,128)(2,1)} %reshape.288) | copy-start | bytes 786436
  85.5 17.7 %all-to-all-start.3 = ((f32[8,4,4096]{2,1,0:T(4,128)}), f32[8,4,4096]{2,1,0:T(4,128)}, u32[]{:S(2)}, u32[]{:S(2)}) async-start(f32[8,4,4096]{2,1,0:T(4,128)} %fusion.12), calls=%async_computation.3 | async-start | bytes 1048576 | tf_op jit(solution)/shard_map/all_to_all | solution.py:69
  105.0 5.8 %collective-permute-start.1 = (bf16[32,4096]{1,0:T(8,128)(2,1)S(1)}, bf16[32,4096]{1,0:T(8,128)(2,1)S(1)}, u32[]{:S(2)}, u32[]{:S(2)}) collective-permute-start(bf16[32,4096]{1,0:T(8,128)(2,1)S(1)} %fusion.6), channel_id=1, source_target_pairs={{0,8},{8,16},{16,24},{24,0},{1,9},{9,17},{17,25},{25,1},{2,10},{10... | collective-permute-start | bytes 786440 | tf_op jit(solution)/shard_map/ppermute | solution.py:12
  128.8 3.2 %copy-start.3 = (bf16[1,384,4096]{2,1,0:T(8,128)(2,1)S(1)}, bf16[1,384,4096]{2,1,0:T(8,128)(2,1)}, u32[]{:S(2)}) copy-start(bf16[1,384,4096]{2,1,0:T(8,128)(2,1)} %param.12) | copy-start | bytes 9437188
  128.8 3.2 %copy-start.7 = (bf16[32,4096]{1,0:T(8,128)(2,1)S(1)}, bf16[32,4096]{1,0:T(8,128)(2,1)}, u32[]{:S(2)}) copy-start(bf16[32,4096]{1,0:T(8,128)(2,1)} %reshape.291) | copy-start | bytes 786436
  134.4 15.0 %all-to-all-start.5 = ((f32[8,4,4096]{2,1,0:T(4,128)}), f32[8,4,4096]{2,1,0:T(4,128)}, u32[]{:S(2)}, u32[]{:S(2)}) async-start(f32[8,4,4096]{2,1,0:T(4,128)} %fusion.10), calls=%async_computation.5 | async-start | bytes 1048576 | tf_op jit(solution)/shard_map/all_to_all | solution.py:69
  151.2 5.8 %collective-permute-start.2 = (bf16[32,4096]{1,0:T(8,128)(2,1)S(1)}, bf16[32,4096]{1,0:T(8,128)(2,1)S(1)}, u32[]{:S(2)}, u32[]{:S(2)}) collective-permute-start(bf16[32,4096]{1,0:T(8,128)(2,1)S(1)} %fusion.5), channel_id=1, source_target_pairs={{0,8},{8,16},{16,24},{24,0},{1,9},{9,17},{17,25},{25,1},{2,10},{10... | collective-permute-start | bytes 786440 | tf_op jit(solution)/shard_map/ppermute | solution.py:12
  176.8 3.2 %copy-start.4 = (bf16[1,384,4096]{2,1,0:T(8,128)(2,1)S(1)}, bf16[1,384,4096]{2,1,0:T(8,128)(2,1)}, u32[]{:S(2)}) copy-start(bf16[1,384,4096]{2,1,0:T(8,128)(2,1)} %param.12) | copy-start | bytes 9437188
  176.8 3.2 %copy-start.8 = (bf16[32,4096]{1,0:T(8,128)(2,1)S(1)}, bf16[32,4096]{1,0:T(8,128)(2,1)}, u32[]{:S(2)}) copy-start(bf16[32,4096]{1,0:T(8,128)(2,1)} %reshape.294) | copy-start | bytes 786436
  182.5 18.4 %all-to-all-start.7 = ((f32[8,4,4096]{2,1,0:T(4,128)}), f32[8,4,4096]{2,1,0:T(4,128)}, u32[]{:S(2)}, u32[]{:S(2)}) async-start(f32[8,4,4096]{2,1,0:T(4,128)} %fusion.8), calls=%async_computation.7 | async-start | bytes 1048576 | tf_op jit(solution)/shard_map/all_to_all | solution.py:69
  202.8 5.8 %collective-permute-start.3 = (bf16[32,4096]{1,0:T(8,128)(2,1)S(1)}, bf16[32,4096]{1,0:T(8,128)(2,1)S(1)}, u32[]{:S(2)}, u32[]{:S(2)}) collective-permute-start(bf16[32,4096]{1,0:T(8,128)(2,1)S(1)} %fusion.4), channel_id=1, source_target_pairs={{0,8},{8,16},{16,24},{24,0},{1,9},{9,17},{17,25},{25,1},{2,10},{10... | collective-permute-start | bytes 786440 | tf_op jit(solution)/shard_map/ppermute | solution.py:12
where the time goes:
time: 211 us; the launch traced here: 209 us
  waiting for transfers between devices  59.8 us (28%)
  blocking collectives  41.6 us (20%)
  other arithmetic  37.6 us (18%)
  matrix products  24.4 us (12%)
  local copies, waits for them, and re-layouts  24.3 us (12%)
  starting transfers between devices  21 us (10%)
    all_to_all x3, blocking collectives, shards(): lax.all_to_all(outgoing, 'ep', split_axis=0, concat_axis=0, tiled=True)  41.6 us
    all_to_all x4, waiting for transfers between devices, shards(): lax.all_to_all(partial_sums, 'ep', split_axis=0, concat_axis=0, tiled=True)  30.9 us
    ppermute x4, waiting for transfers between devices, shifted(): return lax.ppermute(x, axis, [(i, (i + by) % peers) for i in range(peers)])  23 us
    all_to_all x4, starting transfers between devices, shards(): lax.all_to_all(partial_sums, 'ep', split_axis=0, concat_axis=0, tiled=True)  16.7 us
    dot_general x8, matrix products, project_rows(): lax.dot_general(rows, weight_t, (((1,), (1,)), ((), ())), preferred_eleme...  16.7 us
    sort x8, other arithmetic, shards(): order = jnp.argsort(1 - hits, stable=True)[:MOST]  13 us
    gather x8, local copies, waits for them, and re-layouts, shards(): picked.append(normed[order])  10.8 us
    reshape x4, local copies, waits for them, and re-layouts, shards(): flat = block.reshape(senders * slots, width)  6.16 us
  transfers between devices with their start and end apart: 9, of which 9 were waited for; matrix products, arithmetic and copies ran while one was open for 11% of the time, Pallas kernels for 0%

commit v1 on v0

v1 whole, which is shorter than its diff:
```python
import functools

import jax
import jax.numpy as jnp
from jax import lax
from jax.experimental import pallas as pl
from jax.experimental.pallas import tpu as pltpu
from jax.sharding import PartitionSpec as P

FE = 1536
MOST = 4
MESH = pl.DeviceIdType.MESH


def nt_dot(rows, weight_t):
    return lax.dot_general(
        rows, weight_t, (((1,), (1,)), ((), ())), preferred_element_type=jnp.float32
    )


def kernel(
    sections,
    peers,
    sharers,
    ids_ref,
    logits_ref,
    gain_ref,
    hidden_ref,
    wg_hbm,
    wu_hbm,
    wd_hbm,
    out_ref,
    wg,
    wu,
    wd,
    state,
    held_h,
    send_a,
    recv_a,
    send_b,
    recv_b,
    pick,
    comb,
    comb_prev,
    rows_f,
    y_f,
    w_sem,
    sa_sem,
    ra_sem,
    sb_sem,
    rb_sem,
    sh_sem,
    rh_sem,
    c_sem,
    own_sem,
):
    ticks, rows_dev, top = ids_ref.shape
    held = peers // sharers
    sec = lax.axis_index("section")
    me = lax.axis_index("ep")
    after = lax.rem(sec + 1, sections)
    before = lax.rem(sec + sections - 1, sections)

    loads = [
        pltpu.make_async_copy(src, dst, w_sem.at[i])
        for i, (src, dst) in enumerate(((wg_hbm, wg), (wu_hbm, wu), (wd_hbm, wd)))
    ]
    for load in loads:
        load.start()

    barrier = pltpu.get_barrier_semaphore()
    for k in range(peers):
        other = lax.rem(me + k, peers)
        if k:
            pl.semaphore_signal(barrier, inc=1, device_id=(sec, other), device_id_type=MESH)
        pl.semaphore_signal(barrier, inc=1, device_id=(before, other), device_id_type=MESH)

    tri = (
        lax.broadcasted_iota(jnp.int32, (rows_dev, rows_dev), 1)
        < lax.broadcasted_iota(jnp.int32, (rows_dev, rows_dev), 0)
    ).astype(jnp.bfloat16)
    lane = lax.broadcasted_iota(jnp.int32, (rows_dev, 128), 1)
    eye = (
        lax.broadcasted_iota(jnp.int32, (held * MOST, 128), 0) * 1
    )
    eye_row = eye // MOST * (sharers * MOST) + eye % MOST
    eye_bf = (lax.broadcasted_iota(jnp.int32, (held * MOST, 128), 1) == eye_row).astype(
        jnp.bfloat16
    )
    for t in range(ticks):
        ids = ids_ref[t]
        expo = jnp.exp(logits_ref[t])
        probs = expo / jnp.sum(expo, axis=-1, keepdims=True)
        hits = jnp.zeros((rows_dev, 128), jnp.float32)
        weights = jnp.zeros((rows_dev, 128), jnp.float32)
        for j in range(held):
            match = ids == j
            hit = jnp.sum(jnp.where(match, 1.0, 0.0), axis=-1, keepdims=True)
            weight = jnp.sum(jnp.where(match, probs, 0.0), axis=-1, keepdims=True)
            mine = lane // (sharers * MOST) == j
            hits = jnp.where(mine, hit, hits)
            weights = jnp.where(mine, weight, weights)
        place = jnp.dot(tri, hits.astype(jnp.bfloat16), preferred_element_type=jnp.float32)
        slot = lax.rem(lane, MOST).astype(jnp.float32)
        chosen = jnp.where(place == slot, hits, 0.0)
        comb[t] = (chosen * weights.astype(jnp.bfloat16).astype(jnp.float32)).astype(jnp.bfloat16)
        pick[t] = nt_dot(eye_bf, chosen.astype(jnp.bfloat16)).astype(jnp.bfloat16)

    state[0] = hidden_ref[...]
    pl.semaphore_wait(barrier, 2 * peers - 1)
    comb_copy = pltpu.make_async_remote_copy(
        src_ref=comb,
        dst_ref=comb_prev,
        send_sem=c_sem.at[0],
        recv_sem=c_sem.at[1],
        device_id=(after, me),
        device_id_type=MESH,
    )
    comb_copy.start()

    def copy_a(t, k):
        other = lax.rem(me + k, peers)
        return pltpu.make_async_remote_copy(
            src_ref=send_a.at[t, other // sharers],
            dst_ref=recv_a.at[t, me],
            send_sem=sa_sem.at[t, k],
            recv_sem=ra_sem.at[t, k],
            device_id=(sec, other),
            device_id_type=MESH,
        )

    def copy_b(t, k):
        other = lax.rem(me + k, peers)
        return pltpu.make_async_remote_copy(
            src_ref=send_b.at[t, other],
            dst_ref=recv_b.at[t, me],
            send_sem=sb_sem.at[t, k],
            recv_sem=rb_sem.at[t, k],
            device_id=(after, other),
            device_id_type=MESH,
        )

    def copy_h(t):
        return pltpu.make_async_remote_copy(
            src_ref=state.at[t],
            dst_ref=held_h.at[t],
            send_sem=sh_sem.at[t],
            recv_sem=rh_sem.at[t],
            device_id=(after, me),
            device_id_type=MESH,
        )

    def own_a(t):
        return pltpu.make_async_copy(
            send_a.at[t, me // sharers], recv_a.at[t, me], own_sem.at[t]
        )

    far_first = sorted(range(1, peers), key=lambda k: -min(k, peers - k))

    def one_tick(t, first, last):
        hf = state[t].astype(jnp.float32)
        msq = jnp.mean(hf * hf, axis=-1, keepdims=True) + 1e-06
        normed = (hf * lax.rsqrt(msq) * gain_ref[...].astype(jnp.float32)).astype(jnp.bfloat16)
        slots = jnp.dot(pick[t], normed, preferred_element_type=jnp.float32)
        for j in range(held):
            send_a[t, j] = slots[j * MOST : (j + 1) * MOST].astype(jnp.bfloat16)
        for k in far_first:
            copy_a(t, k).start()
        own_a(t).start()
        copy_h(t).start()
        own_a(t).wait()
        for k in range(1, peers):
            copy_a(t, k).wait_recv()
        for p in range(peers):
            rows_f[p * MOST : (p + 1) * MOST, :] = recv_a[t, p].astype(jnp.float32)
        rows = rows_f[...].astype(jnp.bfloat16)

        @pl.when(t == 0)
        def _():
            for load in loads:
                load.wait()

        gate = nt_dot(rows, wg[...])
        upper = nt_dot(rows, wu[...])
        act = (gate / (1.0 + jnp.exp(-gate)) * upper).astype(jnp.bfloat16)
        y_f[...] = jnp.dot(act, wd[...], preferred_element_type=jnp.float32)
        for p in range(peers):
            send_b[t, p] = y_f[p * MOST : (p + 1) * MOST, :].astype(jnp.bfloat16)
        for k in far_first + [0]:
            copy_b(t, k).start()

        @pl.when(t == 0)
        def _():
            comb_copy.wait_recv()

        copy_h(t).wait_recv()
        for k in range(peers):
            copy_b(t, k).wait_recv()
        for p in range(peers):
            rows_f[p * MOST : (p + 1) * MOST, :] = recv_b[t, p].astype(jnp.float32)
        back = rows_f[...].astype(jnp.bfloat16)
        mix = comb_prev[t][:, : peers * MOST]
        out = held_h[t].astype(jnp.float32) + jnp.dot(
            mix, back, preferred_element_type=jnp.float32
        )
        state[t + 1] = out.astype(jnp.bfloat16)

    def body(t, carry):
        one_tick(t, None, None)
        return carry

    lax.fori_loop(0, ticks, body, 0)
    out_ref[...] = state[ticks]

    comb_copy.wait_send()

    def drain(t, carry):
        for k in range(1, peers):
            copy_a(t, k).wait_send()
        for k in range(peers):
            copy_b(t, k).wait_send()
        copy_h(t).wait_send()
        return carry

    lax.fori_loop(0, ticks, drain, 0)


def shards(sections, peers, hidden, route_ids, route_logits, norm_gain, w_gate, w_up, w_down):
    rows_dev, width = hidden.shape
    ticks = route_ids.shape[0]
    units = w_gate.shape[1]
    sharers = FE // units
    held = peers // sharers
    bf = jnp.bfloat16
    vmem = pl.BlockSpec(memory_space=pltpu.VMEM)
    hbm = pl.BlockSpec(memory_space=pl.ANY)
    dma = pltpu.SemaphoreType.DMA
    return pl.pallas_call(
        functools.partial(kernel, sections, peers, sharers),
        out_shape=jax.ShapeDtypeStruct((rows_dev, width), bf),
        in_specs=[vmem] * 4 + [hbm] * 3,
        out_specs=vmem,
        scratch_shapes=[
            pltpu.VMEM((units, width), bf),
            pltpu.VMEM((units, width), bf),
            pltpu.VMEM((units, width), bf),
            pltpu.VMEM((ticks + 1, rows_dev, width), bf),
            pltpu.VMEM((ticks, rows_dev, width), bf),
            pltpu.VMEM((ticks, held, MOST, width), bf),
            pltpu.VMEM((ticks, peers, MOST, width), bf),
            pltpu.VMEM((ticks, peers, MOST, width), bf),
            pltpu.VMEM((ticks, peers, MOST, width), bf),
            pltpu.VMEM((ticks, held * MOST, rows_dev), bf),
            pltpu.VMEM((ticks, rows_dev, 128), bf),
            pltpu.VMEM((ticks, rows_dev, 128), bf),
            pltpu.VMEM((peers * MOST, width), jnp.float32),
            pltpu.VMEM((peers * MOST, width), jnp.float32),
            dma((3,)),
            dma((ticks, peers)),
            dma((ticks, peers)),
            dma((ticks, peers)),
            dma((ticks, peers)),
            dma((ticks,)),
            dma((ticks,)),
            dma((2,)),
            dma((ticks,)),
        ],
        compiler_params=pltpu.CompilerParams(
            collective_id=0, has_side_effects=True, vmem_limit_bytes=56 * 1024 * 1024
        ),
    )(
        route_ids,
        route_logits,
        norm_gain,
        hidden,
        w_gate.reshape(units, width),
        w_up.reshape(units, width),
        w_down.reshape(units, width),
    )


def solution(mesh):
    placed = (
        P(("section", "ep"), None),
        P(None, ("section", "ep"), None),
        P(None, ("section", "ep"), None),
        P("section", None),
        P("section", "ep", None),
        P("section", "ep", None),
        P("section", "ep", None),
    )
    return jax.shard_map(
        functools.partial(shards, mesh.shape["section"], mesh.shape["ep"]),
        mesh=mesh,
        in_specs=placed,
        out_specs=P(("section", "ep"), None),
        check_vma=False,
    )
```

time: 211 us -> 85.1 us (0.40)
  the two profiles are of different devices: /device:TPU:0 before, /device:TPU:17 now
where the time goes in v1:
time: 85.1 us; the launch traced here: 84.8 us
  Pallas kernels  80.2 us (94%)
  local copies, waits for them, and re-layouts  4.51 us (5%)
    pallas_call x1, Pallas kernels, shards(): pl.pallas_call(functools.partial(kernel, sections, peers, sharers), out_s...  80.2 us
    unnamed x3, local copies, waits for them, and re-layouts  4.51 us

profile of v1, /device:TPU:17, one launch (start us, length us, event | category | flops | bytes accessed | tf_op | source)
XLA Modules:
  0.0 84.8 jit_solution(12278135730661623875)
XLA Ops:
  0.0 1.4 %copy.8.ids_ref = s32[4,32,8]{2,1,0:T(8,128)} copy(s32[4,32,8]{1,2,0:T(8,128)} %param.8) | data formatting | bytes 8192 | tf_op args[1]
  1.4 1.4 %copy.9.logits_ref = f32[4,32,8]{2,1,0:T(8,128)} copy(f32[4,32,8]{1,2,0:T(8,128)} %param.9) | data formatting | bytes 8192 | tf_op args[2]
  2.8 80.2 %shard_map.73 = bf16[32,4096]{1,0:T(8,128)(2,1)} custom-call(s32[4,32,8]{2,1,0:T(8,128)} %copy.8.ids_ref, f32[4,32,8]{2,1,0:T(8,128)} %copy.9.logits_ref, bf16[1,4096]{1,0:T(2,128)(2,1)} %gain_ref.1, bf16[32,4096]{1,0:T(8,128)(2,1)} %hidden_ref.1, bf16[384,4096]{1,0:T(8,128)(2,1)} %bitcast.3, bf16[384,4096]{1,0:T(8,128)(2,1)} %bitcast.4, ...), custom_call_target="tpu_custom_call" | custom-call | tf_op jit(solution)/shard_map/pallas_call | solution.py:238
  83.1 1.7 %copy.11 = bf16[32,4096]{1,0:T(8,128)(2,1)} copy(bf16[32,4096]{1,0:T(8,128)(2,1)} %shard_map.73) | data formatting | bytes 524288

commit v2 on v1

v2 whole, which is shorter than its diff:
```python
import functools

import jax
import jax.numpy as jnp
from jax import lax
from jax.experimental import pallas as pl
from jax.experimental.pallas import tpu as pltpu
from jax.sharding import PartitionSpec as P

FE = 1536
MOST = 4
GROUPS = 2
MESH = pl.DeviceIdType.MESH


def nt_dot(rows, weight_t):
    return lax.dot_general(
        rows, weight_t, (((1,), (1,)), ((), ())), preferred_element_type=jnp.float32
    )


def kernel(
    sections,
    peers,
    sharers,
    ids_ref,
    logits_ref,
    gain_ref,
    hidden_ref,
    wg_hbm,
    wu_hbm,
    wd_hbm,
    out_ref,
    wg,
    wu,
    wd,
    state,
    held_h,
    send_a,
    recv_a,
    send_b,
    recv_b,
    pick,
    comb,
    comb_prev,
    rows_f,
    y_f,
    back_f,
    w_sem,
    sa_sem,
    ra_sem,
    sb_sem,
    rb_sem,
    sh_sem,
    rh_sem,
    c_sem,
):
    ticks, top, rows_dev = ids_ref.shape
    held = peers // sharers
    per_expert = sharers * MOST
    sec = lax.axis_index("section")
    me = lax.axis_index("ep")
    after = lax.rem(sec + 1, sections)
    before = lax.rem(sec + sections - 1, sections)

    loads = [
        pltpu.make_async_copy(src, dst, w_sem.at[i])
        for i, (src, dst) in enumerate(((wg_hbm, wg), (wu_hbm, wu), (wd_hbm, wd)))
    ]
    for load in loads:
        load.start()

    def ahead(k):
        return lax.rem(me + k, peers)

    def behind(k):
        return lax.rem(me + peers - k, peers)

    barrier = pltpu.get_barrier_semaphore()
    for k in range(peers):
        if k:
            pl.semaphore_signal(barrier, inc=1, device_id=(sec, ahead(k)), device_id_type=MESH)
        pl.semaphore_signal(barrier, inc=1, device_id=(before, ahead(k)), device_id_type=MESH)

    earlier = (
        lax.broadcasted_iota(jnp.int32, (rows_dev, rows_dev), 0)
        < lax.broadcasted_iota(jnp.int32, (rows_dev, rows_dev), 1)
    ).astype(jnp.bfloat16)
    eye = (
        lax.broadcasted_iota(jnp.int32, (rows_dev, rows_dev), 0)
        == lax.broadcasted_iota(jnp.int32, (rows_dev, rows_dev), 1)
    ).astype(jnp.bfloat16)

    def table(hit_rows, weight_rows, per):
        line = lax.broadcasted_iota(jnp.int32, (held * per, rows_dev), 0)
        hits = jnp.zeros((held * per, rows_dev), jnp.float32)
        weights = jnp.zeros((held * per, rows_dev), jnp.float32)
        for j in range(held):
            hits = jnp.where(line // per == j, hit_rows[j], hits)
            weights = jnp.where(line // per == j, weight_rows[j], weights)
        place = jnp.dot(hits.astype(jnp.bfloat16), earlier, preferred_element_type=jnp.float32)
        slot = lax.rem(line, MOST).astype(jnp.float32)
        chosen = jnp.where(place == slot, hits, 0.0)
        return chosen.astype(jnp.bfloat16), (
            chosen * weights.astype(jnp.bfloat16).astype(jnp.float32)
        ).astype(jnp.bfloat16)

    for t in range(ticks):
        ids = ids_ref[t]
        expo = jnp.exp(logits_ref[t])
        probs = expo / jnp.sum(expo, axis=0, keepdims=True)
        hit_rows = []
        weight_rows = []
        for j in range(held):
            match = ids == j
            hit_rows.append(jnp.sum(jnp.where(match, 1.0, 0.0), axis=0, keepdims=True))
            weight_rows.append(jnp.sum(jnp.where(match, probs, 0.0), axis=0, keepdims=True))
        pick[t] = table(hit_rows, weight_rows, MOST)[0]
        comb[t] = nt_dot(eye, table(hit_rows, weight_rows, per_expert)[1]).astype(jnp.bfloat16)

    state[0] = hidden_ref[...]
    pl.semaphore_wait(barrier, 2 * peers - 1)
    comb_copy = pltpu.make_async_remote_copy(
        src_ref=comb,
        dst_ref=comb_prev,
        send_sem=c_sem.at[0],
        recv_sem=c_sem.at[1],
        device_id=(after, me),
        device_id_type=MESH,
    )
    comb_copy.start()

    def copy_a(t, k):
        return pltpu.make_async_remote_copy(
            src_ref=send_a.at[t, ahead(k) // sharers],
            dst_ref=recv_a.at[t, k],
            send_sem=sa_sem.at[t, k],
            recv_sem=ra_sem.at[t, k],
            device_id=(sec, ahead(k)),
            device_id_type=MESH,
        )

    def copy_b(t, k):
        return pltpu.make_async_remote_copy(
            src_ref=send_b.at[t, k],
            dst_ref=recv_b.at[t, me],
            send_sem=sb_sem.at[t, k],
            recv_sem=rb_sem.at[t, me],
            device_id=(after, behind(k)),
            device_id_type=MESH,
        )

    def came_b(t, i):
        return pltpu.make_async_remote_copy(
            src_ref=send_b.at[t, i],
            dst_ref=recv_b.at[t, i],
            send_sem=sb_sem.at[t, i],
            recv_sem=rb_sem.at[t, i],
            device_id=(after, me),
            device_id_type=MESH,
        )

    def copy_h(t):
        return pltpu.make_async_remote_copy(
            src_ref=state.at[t],
            dst_ref=held_h.at[t],
            send_sem=sh_sem.at[t],
            recv_sem=rh_sem.at[t],
            device_id=(after, me),
            device_id_type=MESH,
        )

    turns = [
        sorted(range(g, peers, GROUPS), key=lambda k: -min(k, peers - k)) for g in range(GROUPS)
    ]

    def one_tick(t, carry):
        hf = state[t].astype(jnp.float32)
        msq = jnp.mean(hf * hf, axis=-1, keepdims=True) + 1e-06
        normed = (hf * lax.rsqrt(msq) * gain_ref[...].astype(jnp.float32)).astype(jnp.bfloat16)
        slots = jnp.dot(pick[t], normed, preferred_element_type=jnp.float32)
        for j in range(held):
            send_a[t, j] = slots[j * MOST : (j + 1) * MOST].astype(jnp.bfloat16)
        for turn in turns:
            for k in turn:
                if k:
                    copy_a(t, k).start()
        copy_h(t).start()

        for g, turn in enumerate(turns):
            for at, k in enumerate(turn):
                if k:
                    copy_a(t, k).wait_recv()
                mine = recv_a[t, k] if k else send_a[t, me // sharers]
                rows_f[g, at * MOST : (at + 1) * MOST, :] = mine.astype(jnp.float32)
            rows = rows_f[g].astype(jnp.bfloat16)
            if g == 0:

                @pl.when(t == 0)
                def _():
                    for load in loads:
                        load.wait()

            gate = nt_dot(rows, wg[...])
            upper = nt_dot(rows, wu[...])
            act = (gate / (1.0 + jnp.exp(-gate)) * upper).astype(jnp.bfloat16)
            y_f[g] = jnp.dot(act, wd[...], preferred_element_type=jnp.float32)
            for at, k in enumerate(turn):
                send_b[t, k] = y_f[g, at * MOST : (at + 1) * MOST, :].astype(jnp.bfloat16)
                copy_b(t, k).start()

        @pl.when(t == 0)
        def _():
            comb_copy.wait_recv()

        copy_h(t).wait_recv()
        for i in range(peers):
            came_b(t, i).wait_recv()
            back_f[i * MOST : (i + 1) * MOST, :] = recv_b[t, i].astype(jnp.float32)
        out = held_h[t].astype(jnp.float32) + jnp.dot(
            comb_prev[t], back_f[...].astype(jnp.bfloat16), preferred_element_type=jnp.float32
        )
        state[t + 1] = out.astype(jnp.bfloat16)
        return carry

    lax.fori_loop(0, ticks, one_tick, 0)
    out_ref[...] = state[ticks]

    comb_copy.wait_send()

    def drain(t, carry):
        for k in range(peers):
            if k:
                copy_a(t, k).wait_send()
            copy_b(t, k).wait_send()
        copy_h(t).wait_send()
        return carry

    lax.fori_loop(0, ticks, drain, 0)


def shards(sections, peers, hidden, route_ids, route_logits, norm_gain, w_gate, w_up, w_down):
    rows_dev, width = hidden.shape
    ticks = route_ids.shape[0]
    units = w_gate.shape[1]
    sharers = FE // units
    held = peers // sharers
    bf = jnp.bfloat16
    vmem = pl.BlockSpec(memory_space=pltpu.VMEM)
    hbm = pl.BlockSpec(memory_space=pl.ANY)
    dma = pltpu.SemaphoreType.DMA
    return pl.pallas_call(
        functools.partial(kernel, sections, peers, sharers),
        out_shape=jax.ShapeDtypeStruct((rows_dev, width), bf),
        in_specs=[vmem] * 4 + [hbm] * 3,
        out_specs=vmem,
        scratch_shapes=[
            pltpu.VMEM((units, width), bf),
            pltpu.VMEM((units, width), bf),
            pltpu.VMEM((units, width), bf),
            pltpu.VMEM((ticks + 1, rows_dev, width), bf),
            pltpu.VMEM((ticks, rows_dev, width), bf),
            pltpu.VMEM((ticks, held, MOST, width), bf),
            pltpu.VMEM((ticks, peers, MOST, width), bf),
            pltpu.VMEM((ticks, peers, MOST, width), bf),
            pltpu.VMEM((ticks, peers, MOST, width), bf),
            pltpu.VMEM((ticks, held * MOST, rows_dev), bf),
            pltpu.VMEM((ticks, rows_dev, peers * MOST), bf),
            pltpu.VMEM((ticks, rows_dev, peers * MOST), bf),
            pltpu.VMEM((GROUPS, peers // GROUPS * MOST, width), jnp.float32),
            pltpu.VMEM((GROUPS, peers // GROUPS * MOST, width), jnp.float32),
            pltpu.VMEM((peers * MOST, width), jnp.float32),
            dma((3,)),
            dma((ticks, peers)),
            dma((ticks, peers)),
            dma((ticks, peers)),
            dma((ticks, peers)),
            dma((ticks,)),
            dma((ticks,)),
            dma((2,)),
        ],
        compiler_params=pltpu.CompilerParams(
            collective_id=0, has_side_effects=True, vmem_limit_bytes=56 * 1024 * 1024
        ),
    )(
        jnp.swapaxes(route_ids, 1, 2),
        jnp.swapaxes(route_logits, 1, 2),
        norm_gain,
        hidden,
        w_gate.reshape(units, width),
        w_up.reshape(units, width),
        w_down.reshape(units, width),
    )


def solution(mesh):
    placed = (
        P(("section", "ep"), None),
        P(None, ("section", "ep"), None),
        P(None, ("section", "ep"), None),
        P("section", None),
        P("section", "ep", None),
        P("section", "ep", None),
        P("section", "ep", None),
    )
    return jax.shard_map(
        functools.partial(shards, mesh.shape["section"], mesh.shape["ep"]),
        mesh=mesh,
        in_specs=placed,
        out_specs=P(("section", "ep"), None),
        check_vma=False,
    )
```

time: 85.1 us -> 75.2 us (0.88)
  the two profiles are of different devices: /device:TPU:17 before, /device:TPU:0 now
where the time goes in v2:
time: 75.2 us; the launch traced here: 74.9 us
  Pallas kernels  73.3 us (97%)
  local copies, waits for them, and re-layouts  1.67 us (2%)
    pallas_call x1, Pallas kernels, shards(): pl.pallas_call(functools.partial(kernel, sections, peers, sharers), out_s...  73.3 us
    unnamed x1, local copies, waits for them, and re-layouts  1.67 us

profile of v2, /device:TPU:0, one launch (start us, length us, event | category | flops | bytes accessed | tf_op | source)
XLA Modules:
  0.0 74.9 jit_solution(824742135114622369)
XLA Ops:
  0.0 73.3 %shard_map.73 = bf16[32,4096]{1,0:T(8,128)(2,1)} custom-call(s32[4,8,32]{2,1,0:T(8,128)} %bitcast.8, f32[4,8,32]{2,1,0:T(8,128)} %bitcast.9, bf16[1,4096]{1,0:T(2,128)(2,1)} %gain_ref.1, bf16[32,4096]{1,0:T(8,128)(2,1)} %hidden_ref.1, bf16[384,4096]{1,0:T(8,128)(2,1)} %bitcast.5, bf16[384,4096]{1,0:T(8,128)(2,1)} %bitcast.6, bf16[384,4096]{1,0:T(8,128)(2,1)} %bitcast.7), custom_call_target="tpu_custom_call" | custom-call | tf_op jit(solution)/shard_map/pallas_call | solution.py:252
  73.3 1.7 %copy.9 = bf16[32,4096]{1,0:T(8,128)(2,1)} copy(bf16[32,4096]{1,0:T(8,128)(2,1)} %shard_map.73) | data formatting | bytes 524288

commit v3 on v2

--- a/solution.py
+++ b/solution.py
@@ -57,7 +57,6 @@
 ):
     ticks, top, rows_dev = ids_ref.shape
     held = peers // sharers
-    per_expert = sharers * MOST
     sec = lax.axis_index("section")
     me = lax.axis_index("ep")
     after = lax.rem(sec + 1, sections)
@@ -91,33 +90,49 @@
         == lax.broadcasted_iota(jnp.int32, (rows_dev, rows_dev), 1)
     ).astype(jnp.bfloat16)
 
-    def table(hit_rows, weight_rows, per):
-        line = lax.broadcasted_iota(jnp.int32, (held * per, rows_dev), 0)
-        hits = jnp.zeros((held * per, rows_dev), jnp.float32)
-        weights = jnp.zeros((held * per, rows_dev), jnp.float32)
-        for j in range(held):
-            hits = jnp.where(line // per == j, hit_rows[j], hits)
-            weights = jnp.where(line // per == j, weight_rows[j], weights)
-        place = jnp.dot(hits.astype(jnp.bfloat16), earlier, preferred_element_type=jnp.float32)
-        slot = lax.rem(line, MOST).astype(jnp.float32)
-        chosen = jnp.where(place == slot, hits, 0.0)
-        return chosen.astype(jnp.bfloat16), (
-            chosen * weights.astype(jnp.bfloat16).astype(jnp.float32)
-        ).astype(jnp.bfloat16)
-
-    for t in range(ticks):
+    turns = [
+        sorted(range(g, peers, GROUPS), key=lambda k: -min(k, peers - k)) for g in reversed(range(GROUPS))
+    ]
+    lines = peers // GROUPS * MOST
+
+    def routing(t):
         ids = ids_ref[t]
         expo = jnp.exp(logits_ref[t])
         probs = expo / jnp.sum(expo, axis=0, keepdims=True)
-        hit_rows = []
-        weight_rows = []
+        matches = [ids == j for j in range(held)]
+        hit_rows = [jnp.sum(jnp.where(m, 1.0, 0.0), axis=0, keepdims=True) for m in matches]
+        weight_rows = [jnp.sum(jnp.where(m, probs, 0.0), axis=0, keepdims=True) for m in matches]
+        return hit_rows, weight_rows
+
+    def choose(hit_rows, expert):
+        shape = (expert.shape[0], rows_dev)
+        hits = jnp.zeros(shape, jnp.float32)
         for j in range(held):
-            match = ids == j
-            hit_rows.append(jnp.sum(jnp.where(match, 1.0, 0.0), axis=0, keepdims=True))
-            weight_rows.append(jnp.sum(jnp.where(match, probs, 0.0), axis=0, keepdims=True))
-        pick[t] = table(hit_rows, weight_rows, MOST)[0]
-        comb[t] = nt_dot(eye, table(hit_rows, weight_rows, per_expert)[1]).astype(jnp.bfloat16)
-
+            hits = jnp.where(expert == j, hit_rows[j], hits)
+        place = jnp.dot(hits.astype(jnp.bfloat16), earlier, preferred_element_type=jnp.float32)
+        slot = lax.rem(lax.broadcasted_iota(jnp.int32, shape, 0), MOST).astype(jnp.float32)
+        return jnp.where(place == slot, hits, 0.0)
+
+    def make_pick(t):
+        expert = lax.broadcasted_iota(jnp.int32, (held * MOST, rows_dev), 0) // MOST
+        pick[t] = choose(routing(t)[0], expert).astype(jnp.bfloat16)
+
+    def make_comb(t):
+        hit_rows, weight_rows = routing(t)
+        for g, turn in enumerate(turns):
+            place = lax.broadcasted_iota(jnp.int32, (lines, rows_dev), 0) // MOST
+            away = jnp.zeros((lines, rows_dev), jnp.int32)
+            for at, k in enumerate(turn):
+                away = jnp.where(place == at, k, away)
+            expert = lax.rem(me + away, peers) // sharers
+            weights = jnp.zeros((lines, rows_dev), jnp.float32)
+            for j in range(held):
+                weights = jnp.where(expert == j, weight_rows[j], weights)
+            rounded = weights.astype(jnp.bfloat16).astype(jnp.float32)
+            scaled = (choose(hit_rows, expert) * rounded).astype(jnp.bfloat16)
+            comb[t, g] = nt_dot(eye, scaled).astype(jnp.bfloat16)
+
+    make_pick(0)
     state[0] = hidden_ref[...]
     pl.semaphore_wait(barrier, 2 * peers - 1)
     comb_copy = pltpu.make_async_remote_copy(
@@ -128,7 +143,6 @@
         device_id=(after, me),
         device_id_type=MESH,
     )
-    comb_copy.start()
 
     def copy_a(t, k):
         return pltpu.make_async_remote_copy(
@@ -143,20 +157,10 @@
     def copy_b(t, k):
         return pltpu.make_async_remote_copy(
             src_ref=send_b.at[t, k],
-            dst_ref=recv_b.at[t, me],
+            dst_ref=recv_b.at[t, k],
             send_sem=sb_sem.at[t, k],
-            recv_sem=rb_sem.at[t, me],
+            recv_sem=rb_sem.at[t, k],
             device_id=(after, behind(k)),
-            device_id_type=MESH,
-        )
-
-    def came_b(t, i):
-        return pltpu.make_async_remote_copy(
-            src_ref=send_b.at[t, i],
-            dst_ref=recv_b.at[t, i],
-            send_sem=sb_sem.at[t, i],
-            recv_sem=rb_sem.at[t, i],
-            device_id=(after, me),
             device_id_type=MESH,
         )
 
@@ -170,15 +174,10 @@
             device_id_type=MESH,
         )
 
-    turns = [
-        sorted(range(g, peers, GROUPS), key=lambda k: -min(k, peers - k)) for g in range(GROUPS)
-    ]
-
     def one_tick(t, carry):
-        hf = state[t].astype(jnp.float32)
+        hf = jnp.dot(pick[t], state[t], preferred_element_type=jnp.float32)
         msq = jnp.mean(hf * hf, axis=-1, keepdims=True) + 1e-06
-        normed = (hf * lax.rsqrt(msq) * gain_ref[...].astype(jnp.float32)).astype(jnp.bfloat16)
-        slots = jnp.dot(pick[t], normed, preferred_element_type=jnp.float32)
+        slots = hf * lax.rsqrt(msq) * gain_ref[...].astype(jnp.float32)
         for j in range(held):
             send_a[t, j] = slots[j * MOST : (j + 1) * MOST].astype(jnp.bfloat16)
         for turn in turns:
@@ -186,6 +185,14 @@
                 if k:
                     copy_a(t, k).start()
         copy_h(t).start()
+
+        @pl.when(t == 0)
+        def _():
+            for later in range(1, ticks):
+                make_pick(later)
+            for each in range(ticks):
+                make_comb(each)
+            comb_copy.start()
 
         for g, turn in enumerate(turns):
             for at, k in enumerate(turn):
@@ -214,12 +221,16 @@
             comb_copy.wait_recv()
 
         copy_h(t).wait_recv()
-        for i in range(peers):
-            came_b(t, i).wait_recv()
-            back_f[i * MOST : (i + 1) * MOST, :] = recv_b[t, i].astype(jnp.float32)
-        out = held_h[t].astype(jnp.float32) + jnp.dot(
-            comb_prev[t], back_f[...].astype(jnp.bfloat16), preferred_element_type=jnp.float32
-        )
+        out = held_h[t].astype(jnp.float32)
+        for g, turn in enumerate(turns):
+            for at, k in enumerate(turn):
+                copy_b(t, k).wait_recv()
+                back_f[g, at * MOST : (at + 1) * MOST, :] = recv_b[t, k].astype(jnp.float32)
+            out = out + jnp.dot(
+                comb_prev[t, g],
+                back_f[g].astype(jnp.bfloat16),
+                preferred_element_type=jnp.float32,
+            )
         state[t + 1] = out.astype(jnp.bfloat16)
         return carry
 
@@ -265,11 +276,11 @@
             pltpu.VMEM((ticks, peers, MOST, width), bf),
             pltpu.VMEM((ticks, peers, MOST, width), bf),
             pltpu.VMEM((ticks, held * MOST, rows_dev), bf),
-            pltpu.VMEM((ticks, rows_dev, peers * MOST), bf),
-            pltpu.VMEM((ticks, rows_dev, peers * MOST), bf),
+            pltpu.VMEM((ticks, GROUPS, rows_dev, peers // GROUPS * MOST), bf),
+            pltpu.VMEM((ticks, GROUPS, rows_dev, peers // GROUPS * MOST), bf),
             pltpu.VMEM((GROUPS, peers // GROUPS * MOST, width), jnp.float32),
             pltpu.VMEM((GROUPS, peers // GROUPS * MOST, width), jnp.float32),
-            pltpu.VMEM((peers * MOST, width), jnp.float32),
+            pltpu.VMEM((GROUPS, peers // GROUPS * MOST, width), jnp.float32),
             dma((3,)),
             dma((ticks, peers)),
             dma((ticks, peers)),

time: 75.2 us -> 73.4 us (0.976)
  Pallas kernels: 73.3 us -> 71.5 us
    pallas_call x1, Pallas kernels: 73.3 us -> 71.5 us  [shards(): pl.pallas_call(functools.partial(kernel, sections, peers, sharers), out_s...]
where the time goes in v3:
time: 73.4 us; the launch traced here: 73.2 us
  Pallas kernels  71.5 us (97%)
  local copies, waits for them, and re-layouts  1.67 us (2%)
    pallas_call x1, Pallas kernels, shards(): pl.pallas_call(functools.partial(kernel, sections, peers, sharers), out_s...  71.5 us
    unnamed x1, local copies, waits for them, and re-layouts  1.67 us

profile of v3, /device:TPU:0, one launch (start us, length us, event | category | flops | bytes accessed | tf_op | source)
XLA Modules:
  0.0 73.2 jit_solution(15365431946543730822)
XLA Ops:
  0.0 71.5 %shard_map.73 = bf16[32,4096]{1,0:T(8,128)(2,1)} custom-call(s32[4,8,32]{2,1,0:T(8,128)} %bitcast.8, f32[4,8,32]{2,1,0:T(8,128)} %bitcast.9, bf16[1,4096]{1,0:T(2,128)(2,1)} %gain_ref.1, bf16[32,4096]{1,0:T(8,128)(2,1)} %hidden_ref.1, bf16[384,4096]{1,0:T(8,128)(2,1)} %bitcast.5, bf16[384,4096]{1,0:T(8,128)(2,1)} %bitcast.6, bf16[384,4096]{1,0:T(8,128)(2,1)} %bitcast.7), custom_call_target="tpu_custom_call" | custom-call | tf_op jit(solution)/shard_map/pallas_call | solution.py:263
  71.5 1.7 %copy.9 = bf16[32,4096]{1,0:T(8,128)(2,1)} copy(bf16[32,4096]{1,0:T(8,128)(2,1)} %shard_map.73) | data formatting | bytes 524288
